TPU v7x, 32 devices: a whole 2x2x4 slice. The times are simulated.
32 devices in a mesh: rows: 4 (over y, x), cols: 8 (over z, core).
Axes of the slice: x: 2, y: 2, z: 4, core: 2. Of those that a mesh axis runs over, the one named last changes fastest.
Arguments:
- tokens: bfloat16 [128, 256, 256], P('rows', 'cols'), may hold values from -45 to 45
- key_bias: bfloat16 [128, 256], P('rows', 'cols'), may hold values from -3 to 250
- cotangent: bfloat16 [128, 256, 256], P('rows', 'cols'), may hold values from -6 to 6
- gain_row: float32 [256], replicated, may hold values from 0.1 to 1.9
- w_qkv_row: bfloat16 [256, 768], replicated, may hold values from -0.375 to 0.375
- w_out_row: bfloat16 [256, 256], replicated, may hold values from -0.375 to 0.375
- gain_col: float32 [256], replicated, may hold values from 0.1 to 1.9
- w_qkv_col: bfloat16 [256, 768], replicated, may hold values from -0.375 to 0.375
- w_out_col: bfloat16 [256, 256], replicated, may hold values from -0.375 to 0.375
- gain_mlp: float32 [256], replicated, may hold values from 0.1 to 1.9
- w_up: bfloat16 [256, 1024], replicated, may hold values from -0.375 to 0.375
- w_down: bfloat16 [1024, 256], replicated, may hold values from -0.1875 to 0.1875
Outputs:
- d_tokens: bfloat16 [128, 256, 256], P('rows', 'cols')
- d_gain_row: float32 [256], replicated
- d_w_qkv_row: float32 [256, 768], replicated
- d_w_out_row: float32 [256, 256], replicated
- d_gain_col: float32 [256], replicated
- d_w_qkv_col: float32 [256, 768], replicated
- d_w_out_col: float32 [256, 256], replicated
- d_gain_mlp: float32 [256], replicated
- d_w_up: float32 [256, 1024], replicated
- d_w_down: float32 [1024, 256], replicated
All inputs are finite; a program needn't handle non-finite values.
Results may differ from a plain program's by a relative error of at most 0.015.
Values may be sent and summed in bfloat16 or wider, within the bound.
No kernel may reach another device: no remote copies, remote signals or barrier semaphores. Data moves between devices by JAX's collectives and lax.ppermute only.
A program may use at most 128 MiB of HBM per device.

v0:
```python
import jax
import jax.numpy as jnp
from jax import lax
from jax.sharding import PartitionSpec as P

HEADS = 4


def product(spec_text, left_op, right_op):
    return jnp.einsum(spec_text, left_op, right_op, preferred_element_type=jnp.float32)


def layer_norm(entries, gain_vec):
    floats = entries.astype(jnp.float32)
    centred = floats - jnp.mean(floats, axis=-1, keepdims=True)
    inverse = lax.rsqrt(jnp.mean(centred * centred, axis=-1, keepdims=True) + 1e-05)
    normed = centred * inverse
    return ((normed * gain_vec).astype(jnp.bfloat16), normed, inverse)


def norm_back(grad_out, normed, inverse, gain_vec):
    scaled = grad_out * gain_vec
    result = inverse * (
        scaled
        - jnp.mean(scaled, axis=-1, keepdims=True)
        - normed * jnp.mean(scaled * normed, axis=-1, keepdims=True)
    )
    gain_grad = jnp.sum((grad_out * normed).reshape(-1, gain_vec.shape[0]), axis=0)
    return (result, gain_grad)


def over_cells(left_op, right_op):
    left_flat = left_op.reshape(-1, left_op.shape[-1])
    right_flat = right_op.reshape(-1, right_op.shape[-1])
    return lax.dot_general(
        left_flat, right_flat, (((0,), (0,)), ((), ())), preferred_element_type=jnp.float32
    )


def times_transpose(entries, weight):
    return lax.dot_general(
        entries, weight, (((entries.ndim - 1,), (1,)), ((), ())), preferred_element_type=jnp.float32
    )


def letters(length_axis):
    if length_axis == 1:
        return ("sqhd,skhd->shqk", "shqk,skhd->sqhd", "shqk,sqhd->skhd")
    return ("qshd,kshd->shqk", "shqk,kshd->qshd", "shqk,qshd->kshd")


def split_heads(packed, head_count):
    features = packed.shape[-1] // 3
    head_shape = packed.shape[:-1] + (head_count, features // head_count)
    return tuple(
        (
            packed[..., member * features : (member + 1) * features].reshape(head_shape)
            for member in range(3)
        )
    )


def key_terms(bias_rows, length_axis):
    floats = bias_rows.astype(jnp.float32)
    if length_axis == 0:
        floats = floats.T
    return floats[:, None, None, :]


def attention_weights(query_block, key_rows, bias_terms, factor, length_axis):
    scores = product(letters(length_axis)[0], query_block, key_rows) * factor + bias_terms
    shifted = jnp.exp(scores - jnp.max(scores, axis=-1, keepdims=True))
    return shifted / jnp.sum(shifted, axis=-1, keepdims=True)


def join_blocks(stacked, length_axis, features):
    if length_axis == 0:
        return stacked.reshape((-1, stacked.shape[2], features))
    reordered = jnp.moveaxis(stacked, 0, 1)
    return reordered.reshape((reordered.shape[0], -1, features))


def attend(packed, bias_rows, head_count, length_axis):
    query_rows, key_rows, value_rows = split_heads(packed, head_count)
    length = packed.shape[length_axis]
    block_len = min(length, 512)
    factor = query_rows.shape[-1] ** (-0.5)
    bias_terms = key_terms(bias_rows, length_axis)
    mixing = letters(length_axis)[1]

    def one_block(offset):
        query_block = lax.dynamic_slice_in_dim(query_rows, offset, block_len, length_axis)
        weights = attention_weights(query_block, key_rows, bias_terms, factor, length_axis)
        return product(mixing, weights.astype(jnp.bfloat16), value_rows).astype(jnp.bfloat16)

    offsets = jnp.arange(length // block_len, dtype=jnp.int32) * block_len
    return join_blocks(lax.map(one_block, offsets), length_axis, packed.shape[-1] // 3)


def attend_back(grad_out, packed, bias_rows, head_count, length_axis):
    query_rows, key_rows, value_rows = split_heads(packed, head_count)
    features = packed.shape[-1] // 3
    grad_heads = grad_out.reshape(query_rows.shape)
    length = packed.shape[length_axis]
    block_len = min(length, 512)
    factor = query_rows.shape[-1] ** (-0.5)
    bias_terms = key_terms(bias_rows, length_axis)
    score_spec, mixing, gather_spec = letters(length_axis)

    def one_block(running, offset):
        key_grad, value_grad = running
        query_block = lax.dynamic_slice_in_dim(query_rows, offset, block_len, length_axis)
        grad_block = lax.dynamic_slice_in_dim(grad_heads, offset, block_len, length_axis)
        weights = attention_weights(query_block, key_rows, bias_terms, factor, length_axis)
        weights_low = weights.astype(jnp.bfloat16)
        weight_grad = product(score_spec, grad_block, value_rows)
        centre = jnp.sum(weights * weight_grad, axis=-1, keepdims=True)
        score_grad = (weights * (weight_grad - centre) * factor).astype(jnp.bfloat16)
        query_grad = product(mixing, score_grad, key_rows)
        key_grad = key_grad + product(gather_spec, score_grad, query_block)
        value_grad = value_grad + product(gather_spec, weights_low, grad_block)
        return ((key_grad, value_grad), query_grad)

    empty_grad = jnp.zeros(key_rows.shape, jnp.float32)
    offsets = jnp.arange(length // block_len, dtype=jnp.int32) * block_len
    (key_grad, value_grad), query_parts = lax.scan(one_block, (empty_grad, empty_grad), offsets)
    query_grad = join_blocks(query_parts, length_axis, features)
    flat_shape = packed.shape[:-1] + (features,)
    joined = jnp.concatenate(
        [query_grad, key_grad.reshape(flat_shape), value_grad.reshape(flat_shape)], axis=-1
    )
    return joined.astype(jnp.bfloat16)


def attention_forward(inputs, bias_rows, gain_vec, w_qkv, w_out, head_count, length_axis):
    normal_in, normed, inverse = layer_norm(inputs, gain_vec)
    packed = jnp.dot(normal_in, w_qkv, preferred_element_type=jnp.float32).astype(jnp.bfloat16)
    mixed_out = attend(packed, bias_rows, head_count, length_axis)
    output = (
        inputs.astype(jnp.float32) + jnp.dot(mixed_out, w_out, preferred_element_type=jnp.float32)
    ).astype(jnp.bfloat16)
    return (output, (normal_in, normed, inverse, packed, mixed_out))


def attention_backward(
    grad_out, saved_parts, bias_rows, gain_vec, w_qkv, w_out, head_count, length_axis
):
    normal_in, normed, inverse, packed, mixed_out = saved_parts
    out_grad = over_cells(mixed_out, grad_out)
    mixed_grad = times_transpose(grad_out, w_out).astype(jnp.bfloat16)
    packed_grad = attend_back(mixed_grad, packed, bias_rows, head_count, length_axis)
    qkv_grad = over_cells(normal_in, packed_grad)
    input_grad, gain_grad = norm_back(
        times_transpose(packed_grad, w_qkv), normed, inverse, gain_vec
    )
    return (
        (grad_out.astype(jnp.float32) + input_grad).astype(jnp.bfloat16),
        (gain_grad, qkv_grad, out_grad),
    )


def feed_backward(inputs, grad_out, gain_vec, w_up, w_down):
    normal_in, normed, inverse = layer_norm(inputs, gain_vec)
    hidden = jnp.dot(normal_in, w_up, preferred_element_type=jnp.float32)
    active, gelu_back = jax.vjp(jax.nn.gelu, hidden)
    active_low = active.astype(jnp.bfloat16)
    down_grad = over_cells(active_low, grad_out)
    hidden_grad = gelu_back(times_transpose(grad_out, w_down))[0].astype(jnp.bfloat16)
    up_grad = over_cells(normal_in, hidden_grad)
    input_grad, gain_grad = norm_back(times_transpose(hidden_grad, w_up), normed, inverse, gain_vec)
    return (
        (grad_out.astype(jnp.float32) + input_grad).astype(jnp.bfloat16),
        (gain_grad, up_grad, down_grad),
    )


def shards(
    tokens,
    key_bias,
    cotangent,
    gain_row,
    w_qkv_row,
    w_out_row,
    gain_col,
    w_qkv_col,
    w_out_col,
    gain_mlp,
    w_up,
    w_down,
):
    row_cells, row_bias = (
        lax.all_to_all(tokens, "cols", split_axis=0, concat_axis=1, tiled=True),
        lax.all_to_all(key_bias, "cols", split_axis=0, concat_axis=1, tiled=True),
    )
    after_rows, row_saved = attention_forward(
        row_cells, row_bias, gain_row, w_qkv_row, w_out_row, HEADS, 1
    )
    column_cells = lax.all_to_all(
        lax.all_to_all(after_rows, "cols", split_axis=1, concat_axis=0, tiled=True),
        "rows",
        split_axis=1,
        concat_axis=0,
        tiled=True,
    )
    column_grads, column_bias = (
        lax.all_to_all(cotangent, "rows", split_axis=1, concat_axis=0, tiled=True),
        lax.all_to_all(key_bias, "rows", split_axis=1, concat_axis=0, tiled=True),
    )
    after_cols, column_saved = attention_forward(
        column_cells, column_bias, gain_col, w_qkv_col, w_out_col, HEADS, 0
    )
    mid_grad, feed_grads = feed_backward(after_cols, column_grads, gain_mlp, w_up, w_down)
    cell_grad, attn_grads = attention_backward(
        mid_grad, column_saved, column_bias, gain_col, w_qkv_col, w_out_col, HEADS, 0
    )
    factor = float(
        tokens.shape[0] * tokens.shape[1] * lax.axis_size("rows") * lax.axis_size("cols")
    ) ** (-0.5)
    other_sums = tuple((grad_term * factor for grad_term in attn_grads + feed_grads))
    grad_rows = lax.all_to_all(
        lax.all_to_all(cell_grad, "rows", split_axis=0, concat_axis=1, tiled=True),
        "cols",
        split_axis=0,
        concat_axis=1,
        tiled=True,
    )
    token_grad_rows, row_grads = attention_backward(
        grad_rows, row_saved, row_bias, gain_row, w_qkv_row, w_out_row, HEADS, 1
    )
    d_tokens = lax.all_to_all(token_grad_rows, "cols", split_axis=1, concat_axis=0, tiled=True)
    row_sums = tuple((grad_term * factor for grad_term in row_grads))
    summed = lax.psum(
        (
            row_sums[0],
            row_sums[1],
            row_sums[2],
            other_sums[0],
            other_sums[1],
            other_sums[2],
            other_sums[3],
            other_sums[4],
            other_sums[5],
        ),
        ("rows", "cols"),
    )
    row_sums = summed[:3]
    other_sums = summed[3:]
    return (
        d_tokens,
        row_sums[0],
        row_sums[1],
        row_sums[2],
        other_sums[0],
        other_sums[1],
        other_sums[2],
        other_sums[3],
        other_sums[4],
        other_sums[5],
    )


def solution(mesh):
    in_specs = (
        P("rows", "cols", None),
        P("rows", "cols"),
        P("rows", "cols", None),
        P(),
        P(),
        P(),
        P(),
        P(),
        P(),
        P(),
        P(),
        P(),
    )
    out_specs = (P("rows", "cols", None), P(), P(), P(), P(), P(), P(), P(), P(), P())
    return jax.shard_map(shards, mesh=mesh, in_specs=in_specs, out_specs=out_specs, check_vma=False)
```

profile of v0, /device:TPU:0, one launch (start us, length us, event | category | flops | bytes accessed | tf_op | source)
XLA Modules:
  0.0 385.8 jit_solution(3843586543527307721)
XLA Ops:
  7.2 12.1 %all_to_all.134 = bf16[8,4,32]{2,1,0:T(4,128)(2,1)S(1)} all-to-all(bf16[8,4,32]{2,1,0:T(4,128)(2,1)} %bitcast.263), channel_id=1, replica_groups=mesh['rows'=4,'cols'=8] {'cols'}, dimensions={0} | all-to-all | bytes 4096 | tf_op jit(solution)/shard_map/all_to_all | solution.py:193
  19.3 3.6 all-to-all-start.1
  24.4 13.7 %all-to-all-done.1 = bf16[32,32,256]{2,1,0:T(8,128)(2,1)S(1)} async-done(((bf16[32,32,256]{2,1,0:T(8,128)(2,1)}), bf16[32,32,256]{2,1,0:T(8,128)(2,1)S(1)}, u32[]{:S(2)}, u32[]{:S(2)}) %all-to-all-start.1) | async-done | bytes 524320 | tf_op jit(solution)/shard_map/all_to_all | solution.py:192
  38.2 3.7 all-to-all-start.5
  46.3 4.7 %fusion.124 = (f32[4,4,256]{2,1,0:T(4,128)S(1)}, f32[4,4,256,256]{2,3,1,0:T(8,128)}) fusion(f32[4,256]{1,0:T(4,128)S(1)} %reshape.252, bf16[4,256,4,64]{1,3,2,0:T(8,128)(2,1)S(1)} %bitcast.249, bf16[4,256,4,64]{1,3,2,0:T(8,128)(2,1)} %bitcast.247), kind=kOutput, calls=%fused_computation.165 | convolution fusion | flops 138412288 | bytes 5263360 | tf_op jit(solution)/shard_map/while/body/eval_jaxpr/sub | solution.py:72
  51.0 2.7 convolution_convert_fusion.7
  56.1 3.5 all-to-all-start.3
  60.7 14.2 %all-to-all-done.3 = bf16[4,256,256]{2,0,1:T(4,128)(2,1)S(1)} async-done(((bf16[4,256,256]{2,0,1:T(4,128)(2,1)}), bf16[4,256,256]{2,0,1:T(4,128)(2,1)S(1)}, u32[]{:S(2)}, u32[]{:S(2)}) %all-to-all-start.3) | async-done | bytes 524320 | tf_op jit(solution)/shard_map/all_to_all | solution.py:199
  74.8 4.2 %all-to-all-start = ((bf16[32,32,256]{2,0,1:T(8,128)(2,1)}), bf16[32,32,256]{2,0,1:T(8,128)(2,1)S(1)}, u32[]{:S(2)}, u32[]{:S(2)}) async-start(bf16[32,32,256]{2,0,1:T(8,128)(2,1)} %copy.364), calls=%async_computation | async-start | bytes 1048576 | tf_op jit(solution)/shard_map/all_to_all | solution.py:206
  80.2 6.6 %all-to-all-done = bf16[32,32,256]{2,0,1:T(8,128)(2,1)S(1)} async-done(((bf16[32,32,256]{2,0,1:T(8,128)(2,1)}), bf16[32,32,256]{2,0,1:T(8,128)(2,1)S(1)}, u32[]{:S(2)}, u32[]{:S(2)}) %all-to-all-start) | async-done | bytes 524320 | tf_op jit(solution)/shard_map/all_to_all | solution.py:206
  86.9 3.7 all-to-all-start.4
  91.5 5.8 %all-to-all-done.4 = bf16[32,32,256]{2,0,1:T(8,128)(2,1)S(1)} async-done(((bf16[32,32,256]{2,0,1:T(8,128)(2,1)}), bf16[32,32,256]{2,0,1:T(8,128)(2,1)S(1)}, u32[]{:S(2)}, u32[]{:S(2)}) %all-to-all-start.4) | async-done | bytes 524320 | tf_op jit(solution)/shard_map/all_to_all | solution.py:198
  100.8 1.6 convolution_convert_fusion
  103.5 2.0 copy.387
  107.9 3.7 fusion.125
  111.6 2.0 convolution_convert_fusion.6
  115.3 2.8 multiply_convert_fusion
  118.2 3.2 fusion.10
  125.3 2.0 copy.392
  127.3 3.5 convolution_convert_fusion.5
  130.8 1.8 fusion.126
  132.6 5.2 %fusion.42 = bf16[8,4,64,128]{3,2,1,0:T(8,128)(2,1)} fusion(bf16[128,8,4,64]{0,3,2,1:T(8,128)(2,1)} %bitcast.252, f32[8,4,128,128]{2,3,1,0:T(8,128)} %fusion.126, f32[8,4,128,128]{2,3,1,0:T(8,128)} %get-tuple-element.127, f32[8,4,128]{2,1,0:T(4,128)S(1)} %get-tuple-element.126), kind=kOutput, calls=%fused_computation.49 | convolution fusion | flops 71045248 | bytes 5259264 | tf_op jit(solution)/shard_map/while/body/eval_jaxpr/shqk,kshd->qshd/dot_general | solution.py:10
  137.9 5.0 %fusion.45 = bf16[8,4,64,128]{3,2,1,0:T(8,128)(2,1)} fusion(bf16[128,8,4,64]{0,3,2,1:T(8,128)(2,1)S(1)} %bitcast.254, f32[8,4,128,128]{2,3,1,0:T(8,128)} %fusion.126, f32[8,4,128,128]{2,3,1,0:T(8,128)} %get-tuple-element.127, f32[8,4,128]{2,1,0:T(4,128)S(1)} %get-tuple-element.126), kind=kOutput, calls=%fused_computation.50 | convolution fusion | flops 71045248 | bytes 5259264 | tf_op jit(solution)/shard_map/while/body/eval_jaxpr/shqk,qshd->kshd/dot_general | solution.py:10
  144.1 2.2 copy.397
  146.4 2.0 copy.396
  148.4 3.2 multiply_reduce_fusion.2
  153.6 4.1 %all-to-all-start.6 = ((bf16[128,8,256]{2,1,0:T(8,128)(2,1)}), bf16[128,8,256]{2,1,0:T(8,128)(2,1)}, u32[]{:S(2)}, u32[]{:S(2)}) async-start(bf16[128,8,256]{2,1,0:T(8,128)(2,1)} %copy.399), calls=%async_computation.6 | async-start | bytes 1048576 | tf_op jit(solution)/shard_map/all_to_all | solution.py:221
  160.1 1.8 copy.416
  164.3 1.9 copy.454
  166.3 3.5 all-to-all-start.7
  170.1 2.3 convolution_multiply_fusion
  172.3 3.0 fusion.56
  175.3 2.0 fusion.38
  177.3 2.4 fusion.39
  179.7 5.3 %all-to-all-done.7 = bf16[32,32,256]{2,1,0:T(8,128)(2,1)S(1)} async-done(((bf16[32,32,256]{2,1,0:T(8,128)(2,1)}), bf16[32,32,256]{2,1,0:T(8,128)(2,1)S(1)}, u32[]{:S(2)}, u32[]{:S(2)}) %all-to-all-start.7) | async-done | bytes 524320 | tf_op jit(solution)/shard_map/all_to_all | solution.py:220
  185.4 3.8 convolution_convert_fusion.4
  189.3 2.7 fusion.127
  192.0 8.0 %fusion.48 = bf16[4,4,64,256]{3,2,1,0:T(8,128)(2,1)} fusion(bf16[4,256,4,64]{1,3,2,0:T(8,128)(2,1)S(1)} %bitcast.248, f32[4,4,256,256]{2,3,1,0:T(8,128)} %fusion.127, f32[4,4,256,256]{2,3,1,0:T(8,128)} %get-tuple-element.125, f32[4,4,256]{2,1,0:T(4,128)S(1)} %get-tuple-element.124), kind=kOutput, calls=%fused_computation.51 | convolution fusion | flops 141824256 | bytes 9453568 | tf_op jit(solution)/shard_map/while/body/eval_jaxpr/shqk,skhd->sqhd/dot_general | solution.py:10
  200.0 8.0 %fusion.51 = bf16[4,4,64,256]{3,2,1,0:T(8,128)(2,1)} fusion(bf16[4,256,4,64]{1,3,2,0:T(8,128)(2,1)S(1)} %bitcast.250, f32[4,4,256,256]{2,3,1,0:T(8,128)} %fusion.127, f32[4,4,256,256]{2,3,1,0:T(8,128)} %get-tuple-element.125, f32[4,4,256]{2,1,0:T(4,128)S(1)} %get-tuple-element.124), kind=kOutput, calls=%fused_computation.52 | convolution fusion | flops 141824256 | bytes 9453568 | tf_op jit(solution)/shard_map/while/body/eval_jaxpr/shqk,sqhd->skhd/dot_general | solution.py:10
  209.3 2.1 copy.406
  211.4 2.0 copy.405
  214.5 2.7 fusion.57
  221.9 3.5 all-to-all-start.8
  225.4 41.2 %all-reduce = (f32[256]{0:T(256)}, f32[256]{0:T(256)}, f32[256]{0:T(256)}) all-reduce(f32[256]{0:T(256)S(1)} %broadcast_multiply_fusion.11, f32[256]{0:T(256)S(1)} %broadcast_multiply_fusion.10, f32[256]{0:T(256)S(1)} %broadcast_multiply_fusion.9), channel_id=1, replica_groups=mesh['rows'=4,'cols'=8] {'rows','cols'}, use_global_device_ids=true, to_apply=%region_19.20 | all-reduce | flops 768 | bytes 6144 | tf_op jit(solution)/shard_map/psum | solution.py:232
  267.6 102.7 %all-reduce.4.cloned.1.call-done = (f32[256,768]{1,0:T(8,128)}, f32[256,256]{1,0:T(8,128)}, f32[256,768]{1,0:T(8,128)}, f32[256,256]{1,0:T(8,128)}, f32[256,1024]{1,0:T(8,128)}, /*index=5*/f32[1024,256]{1,0:T(8,128)}) async-done(((f32[256,768]{1,0:T(8,128)}, f32[256,256]{1,0:T(8,128)}, f32[256,768]{1,0:T(8,128)}, f32[256,256]{1,0:T(8,128)}, f32[256,1024]{1,0:T(8,128)}, /*index=5*/f32[1024,256]{1,0:T(8,128)}), ...) | async-done | bytes 4194320 | tf_op jit(solution)/shard_map/psum | solution.py:232
  370.2 2.2 copy.461
  372.5 1.7 copy.462
  374.2 2.1 copy.463
  (178 shorter events, 43.2 us)
Async XLA Ops:
  7.2 108.1 %copy-start = (bf16[256,1024]{1,0:T(8,128)(2,1)S(1)}, bf16[256,1024]{1,0:T(8,128)(2,1)}, u32[]{:S(2)}) copy-start(bf16[256,1024]{1,0:T(8,128)(2,1)} %param.22) | copy-start | bytes 1572868
  19.3 23.7 %copy-start.41 = (f32[256]{0:T(256)S(1)}, f32[256]{0:T(256)}, u32[]{:S(2)}) copy-start(f32[256]{0:T(256)} %param.15) | copy-start | bytes 3076
  19.3 18.9 %all-to-all-start.1 = ((bf16[32,32,256]{2,1,0:T(8,128)(2,1)}), bf16[32,32,256]{2,1,0:T(8,128)(2,1)S(1)}, u32[]{:S(2)}, u32[]{:S(2)}) async-start(bf16[32,32,256]{2,1,0:T(8,128)(2,1)} %param.12), calls=%async_computation.1 | async-start | bytes 1048576 | tf_op jit(solution)/shard_map/all_to_all | solution.py:192
  38.2 17.9 %all-to-all-start.5 = ((bf16[4,2,128]{2,1,0:T(2,128)(2,1)}), bf16[4,2,128]{2,1,0:T(2,128)(2,1)S(1)}, u32[]{:S(2)}, u32[]{:S(2)}) async-start(bf16[4,2,128]{2,1,0:T(2,128)(2,1)} %reshape.268), calls=%async_computation.5 | async-start | bytes 4096 | tf_op jit(solution)/shard_map/all_to_all | solution.py:207
  41.9 2.2 copy-start.36
  46.0 4.9 %copy-start.29 = (bf16[4,256,256]{1,2,0:T(8,128)(2,1)}, bf16[4,256,256]{1,2,0:T(8,128)(2,1)S(1)}, u32[]{:S(2)}) copy-start(bf16[4,256,256]{1,2,0:T(8,128)(2,1)S(1)} %copy.369) | copy-start | bytes 1572868
  46.2 4.7 %copy-start.8 = (bf16[4,256,256]{1,2,0:T(8,128)(2,1)}, bf16[4,256,256]{1,2,0:T(8,128)(2,1)S(1)}, u32[]{:S(2)}) copy-start(bf16[4,256,256]{1,2,0:T(8,128)(2,1)S(1)} %copy.368) | copy-start | bytes 1572868
  50.9 3.6 copy-start.26
  53.7 5.9 %copy-start.27 = (bf16[32,32,256]{2,1,0:T(8,128)(2,1)S(1)}, bf16[32,32,256]{2,1,0:T(8,128)(2,1)}, u32[]{:S(2)}) copy-start(bf16[32,32,256]{2,1,0:T(8,128)(2,1)} %param.14) | copy-start | bytes 1572868
  56.1 18.8 %all-to-all-start.3 = ((bf16[4,256,256]{2,0,1:T(4,128)(2,1)}), bf16[4,256,256]{2,0,1:T(4,128)(2,1)S(1)}, u32[]{:S(2)}, u32[]{:S(2)}) async-start(bf16[4,256,256]{2,0,1:T(4,128)(2,1)} %copy.374), calls=%async_computation.3 | async-start | bytes 1048576 | tf_op jit(solution)/shard_map/all_to_all | solution.py:199
  74.8 12.0 %all-to-all-start = ((bf16[32,32,256]{2,0,1:T(8,128)(2,1)}), bf16[32,32,256]{2,0,1:T(8,128)(2,1)S(1)}, u32[]{:S(2)}, u32[]{:S(2)}) async-start(bf16[32,32,256]{2,0,1:T(8,128)(2,1)} %copy.364), calls=%async_computation | async-start | bytes 1048576 | tf_op jit(solution)/shard_map/all_to_all | solution.py:206
  86.9 11.8 %copy-start.2 = (bf16[32,32,256]{2,0,1:T(8,128)(2,1)}, bf16[32,32,256]{2,0,1:T(8,128)(2,1)S(1)}, u32[]{:S(2)}) copy-start(bf16[32,32,256]{2,0,1:T(8,128)(2,1)S(1)} %all-to-all-done) | copy-start | bytes 1572868
  86.9 10.4 %all-to-all-start.4 = ((bf16[32,32,256]{2,0,1:T(8,128)(2,1)}), bf16[32,32,256]{2,0,1:T(8,128)(2,1)S(1)}, u32[]{:S(2)}, u32[]{:S(2)}) async-start(bf16[32,32,256]{2,0,1:T(8,128)(2,1)} %copy.377), calls=%async_computation.4 | async-start | bytes 1048576 | tf_op jit(solution)/shard_map/all_to_all | solution.py:198
  90.7 8.9 %copy-start.40 = (f32[256]{0:T(256)S(1)}, f32[256]{0:T(256)}, u32[]{:S(2)}) copy-start(f32[256]{0:T(256)} %param.18) | copy-start | bytes 3076
  107.9 5.8 %copy-start.20 = (bf16[128,8,256]{0,2,1:T(8,128)(2,1)}, bf16[128,8,256]{0,2,1:T(8,128)(2,1)S(1)}, u32[]{:S(2)}) copy-start(bf16[128,8,256]{0,2,1:T(8,128)(2,1)S(1)} %copy.385) | copy-start | bytes 1572868
  111.6 2.9 copy-start.25
  111.6 3.8 copy-start.39
  115.3 2.8 copy-start.12
  115.3 2.8 copy-start.44
  121.4 2.0 copy-start.13
  127.3 3.5 copy-start.21
  127.3 3.5 copy-start.22
  132.6 5.2 %copy-start.32 = (bf16[128,8,256]{0,2,1:T(8,128)(2,1)S(1)}, bf16[128,8,256]{0,2,1:T(8,128)(2,1)}, u32[]{:S(2)}) copy-start(bf16[128,8,256]{0,2,1:T(8,128)(2,1)} %copy.386) | copy-start | bytes 1572868
  144.1 4.3 %copy-start.31 = (bf16[128,8,256]{2,0,1:T(8,128)(2,1)}, bf16[128,8,256]{2,0,1:T(8,128)(2,1)S(1)}, u32[]{:S(2)}) copy-start(bf16[128,8,256]{2,0,1:T(8,128)(2,1)S(1)} %copy.398) | copy-start | bytes 1572868
  148.4 3.2 copy-start.5
  151.6 6.1 %copy-start.3 = (bf16[32,32,256]{2,0,1:T(8,128)(2,1)S(1)}, bf16[32,32,256]{2,0,1:T(8,128)(2,1)}, u32[]{:S(2)}) copy-start(bf16[32,32,256]{2,0,1:T(8,128)(2,1)} %copy-done.2) | copy-start | bytes 1572868
  152.5 6.3 %copy-start.11 = (bf16[4,4,64,256]{3,2,1,0:T(8,128)(2,1)S(1)}, bf16[4,4,64,256]{3,2,1,0:T(8,128)(2,1)}, u32[]{:S(2)}) copy-start(bf16[4,4,64,256]{3,2,1,0:T(8,128)(2,1)} %copy-done.10) | copy-start | bytes 1572868
  153.6 10.8 %all-to-all-start.6 = ((bf16[128,8,256]{2,1,0:T(8,128)(2,1)}), bf16[128,8,256]{2,1,0:T(8,128)(2,1)}, u32[]{:S(2)}, u32[]{:S(2)}) async-start(bf16[128,8,256]{2,1,0:T(8,128)(2,1)} %copy.399), calls=%async_computation.6 | async-start | bytes 1048576 | tf_op jit(solution)/shard_map/all_to_all | solution.py:221
  159.2 10.9 %copy-start.6 = (bf16[128,8,256]{2,0,1:T(8,128)(2,1)S(1)}, bf16[128,8,256]{2,0,1:T(8,128)(2,1)}, u32[]{:S(2)}) copy-start(bf16[128,8,256]{2,0,1:T(8,128)(2,1)} %copy-done.4) | copy-start | bytes 1572868
  163.5 8.9 %copy-start.18 = (bf16[128,8,256]{2,0,1:T(8,128)(2,1)S(1)}, bf16[128,8,256]{2,0,1:T(8,128)(2,1)}, u32[]{:S(2)}) copy-start(bf16[128,8,256]{2,0,1:T(8,128)(2,1)} %copy-done.17) | copy-start | bytes 1572868
  166.3 18.8 %all-to-all-start.7 = ((bf16[32,32,256]{2,1,0:T(8,128)(2,1)}), bf16[32,32,256]{2,1,0:T(8,128)(2,1)S(1)}, u32[]{:S(2)}, u32[]{:S(2)}) async-start(bf16[32,32,256]{2,1,0:T(8,128)(2,1)} %bitcast.239), calls=%async_computation.7 | async-start | bytes 1048576 | tf_op jit(solution)/shard_map/all_to_all | solution.py:220
  169.8 200.5 %all-reduce.4.cloned.1.call-start = ((), (), s32[]{:S(2)}) async-start(), calls=%async_computation.9 | async-start | bytes 8388608 | tf_op jit(solution)/shard_map/psum | solution.py:232
  172.3 3.0 copy-start.14
  175.3 2.0 copy-start.33
  175.3 2.0 copy-start.45
  185.4 3.8 copy-start.9
  189.3 2.7 copy-start.28
  192.0 8.0 %copy-start.30 = (bf16[4,256,256]{1,2,0:T(8,128)(2,1)S(1)}, bf16[4,256,256]{1,2,0:T(8,128)(2,1)}, u32[]{:S(2)}) copy-start(bf16[4,256,256]{1,2,0:T(8,128)(2,1)} %copy-done.29) | copy-start | bytes 1572868
  208.0 5.5 %copy-start.19 = (bf16[32,8,4,256]{3,1,2,0:T(8,128)(2,1)S(1)}, bf16[32,8,4,256]{3,1,2,0:T(8,128)(2,1)}, u32[]{:S(2)}) copy-start(bf16[32,8,4,256]{3,1,2,0:T(8,128)(2,1)} %copy.437) | copy-start | bytes 1572868
  208.0 6.5 %copy-start.16 = (bf16[4,256,256]{2,1,0:T(8,128)(2,1)S(1)}, bf16[4,256,256]{2,1,0:T(8,128)(2,1)}, u32[]{:S(2)}) copy-start(bf16[4,256,256]{2,1,0:T(8,128)(2,1)} %copy-done.15) | copy-start | bytes 1572868
  217.2 1.3 copy-start.37
  219.8 5.6 %copy-start.42 = (f32[256]{0:T(256)S(1)}, f32[256]{0:T(256)}, u32[]{:S(2)}) copy-start(f32[256]{0:T(256)} %get-tuple-element.73) | copy-start | bytes 3076
  219.8 5.6 %copy-start.43 = (f32[256]{0:T(256)S(1)}, f32[256]{0:T(256)}, u32[]{:S(2)}) copy-start(f32[256]{0:T(256)} %get-tuple-element.84) | copy-start | bytes 3076
  221.9 44.8 %all-to-all-start.8 = ((bf16[4,256,256]{2,0,1:T(4,128)(2,1)}), bf16[4,256,256]{2,0,1:T(4,128)(2,1)S(1)}, u32[]{:S(2)}, u32[]{:S(2)}) async-start(bf16[4,256,256]{2,0,1:T(4,128)(2,1)} %copy.409), calls=%async_computation.8 | async-start | bytes 1048576 | tf_op jit(solution)/shard_map/all_to_all | solution.py:230
  370.2 6.0 %copy-start.38 = (f32[256,256]{1,0:T(8,128)S(1)}, f32[256,256]{1,0:T(8,128)}, u32[]{:S(2)}) copy-start(f32[256,256]{1,0:T(8,128)} %get-tuple-element.143) | copy-start | bytes 786436
  370.2 6.7 %copy-start.24 = (f32[256,1024]{1,0:T(8,128)S(1)}, f32[256,1024]{1,0:T(8,128)}, u32[]{:S(2)}) copy-start(f32[256,1024]{1,0:T(8,128)} %get-tuple-element.145) | copy-start | bytes 3145732
  370.2 7.7 %copy-start.23 = (f32[1024,256]{1,0:T(8,128)S(1)}, f32[1024,256]{1,0:T(8,128)}, u32[]{:S(2)}) copy-start(f32[1024,256]{1,0:T(8,128)} %get-tuple-element.146) | copy-start | bytes 3145732
  372.5 6.4 %copy-start.1 = (bf16[256,1024]{1,0:T(8,128)(2,1)S(1)}, bf16[256,1024]{1,0:T(8,128)(2,1)}, u32[]{:S(2)}) copy-start(bf16[256,1024]{1,0:T(8,128)(2,1)} %param.22) | copy-start | bytes 1572868
  (7 other events, 6.3 us)
Sparse Core Ops, SparseCore 0:
  217.3 152.8 all-reduce.3
where the time goes:
time: 387 us; the launch traced here: 386 us
  waiting for transfers between devices  149 us (39%)
  matrix products  80.4 us (21%)
  blocking collectives  53.3 us (14%)
  local copies, waits for them, and re-layouts  52.3 us (14%)
  starting transfers between devices  30.1 us (8%)
  between operations  14.7 us (4%)
  other arithmetic  5.81 us (2%)
    psum x1, waiting for transfers between devices, shards(): lax.psum((row_sums[0], row_sums[1], row_sums[2], other_sums[0], other_sum...  103 us
    dot_general x10, matrix products, product(): jnp.einsum(spec_text, left_op, right_op, preferred_element_type=jnp.float32)  42.8 us
    psum x1, blocking collectives, shards(): lax.psum((row_sums[0], row_sums[1], row_sums[2], other_sums[0], other_sum...  41.2 us
    unnamed x104, local copies, waits for them, and re-layouts  17.6 us
    all_to_all x1, waiting for transfers between devices, shards(): lax.all_to_all(after_rows, 'cols', split_axis=1, concat_axis=0, tiled=True)  14.2 us
    all_to_all x1, waiting for transfers between devices, shards(): lax.all_to_all(tokens, 'cols', split_axis=0, concat_axis=1, tiled=True)  13.7 us
    dot_general x6, matrix products, over_cells(): lax.dot_general(left_flat, right_flat, (((0,), (0,)), ((), ())), preferre...  13.3 us
    all_to_all x1, blocking collectives, shards(): lax.all_to_all(key_bias, 'cols', split_axis=0, concat_axis=1, tiled=True)  12.1 us
  transfers between devices with their start and end apart: 9, of which 7 were waited for; matrix products, arithmetic and copies ran while one was open for 10% of the time, Pallas kernels for 0%

commit v1 on v0

--- a/solution.py
+++ b/solution.py
@@ -4,6 +4,29 @@
 from jax.sharding import PartitionSpec as P
 
 HEADS = 4
+
+
+def cut_along(value, dim, size):
+    shape = value.shape
+    blocks = value.reshape(*shape[:dim], size, shape[dim] // size, *shape[dim + 1 :])
+    return jnp.moveaxis(blocks, dim, 0)
+
+
+def joined_along(tiles, dim):
+    tiles = jnp.moveaxis(tiles, 0, dim)
+    dims = tiles.shape
+    return tiles.reshape(*dims[:dim], dims[dim] * dims[dim + 1], *dims[dim + 2 :])
+
+
+def exchange_in_pairs(shard, axis, split_dim, concat_dim):
+    size, position = (lax.axis_size(axis), lax.axis_index(axis))
+    parts = cut_along(shard, split_dim, size)
+    outs = [parts[position]]
+    for step in range(1, size):
+        sent = parts[position ^ step]
+        outs.append(lax.ppermute(sent, axis, [(i, i ^ step) for i in range(size)]))
+    parts = jnp.stack(outs)[position ^ jnp.arange(size)]
+    return joined_along(parts, concat_dim)
 
 
 def product(spec_text, left_op, right_op):
@@ -203,7 +226,7 @@
         tiled=True,
     )
     column_grads, column_bias = (
-        lax.all_to_all(cotangent, "rows", split_axis=1, concat_axis=0, tiled=True),
+        exchange_in_pairs(cotangent, "rows", 1, 0),
         lax.all_to_all(key_bias, "rows", split_axis=1, concat_axis=0, tiled=True),
     )
     after_cols, column_saved = attention_forward(

time: 387 us -> 380 us (0.982)
  waiting for transfers between devices: 149 us -> 143 us
    all_to_all x1 -> x0, waiting for transfers between devices: 6.62 us -> none  [shards(): lax.all_to_all(cotangent, 'rows', split_axis=1, concat_axis=0, tiled=True)]
    all_to_all x1 -> x0, starting transfers between devices: 4.19 us -> none  [shards(): lax.all_to_all(cotangent, 'rows', split_axis=1, concat_axis=0, tiled=True)]
    unnamed x104 -> x91, local copies, waits for them, and re-layouts: 17.6 us -> 15 us
  transfers between devices with their start and end apart: 9 -> 11, of which waited for: 7 -> 7; matrix products, arithmetic and copies ran while one was open for 10% -> 6% of each run, Pallas kernels for 0% -> 0%
where the time goes in v1:
time: 380 us; the launch traced here: 378 us
  waiting for transfers between devices  143 us (38%)
  matrix products  80.7 us (21%)
  blocking collectives  53.2 us (14%)
  local copies, waits for them, and re-layouts  51.1 us (13%)
  starting transfers between devices  29.5 us (8%)
  between operations  14.7 us (4%)
  other arithmetic  5.88 us (2%)
    psum x1, waiting for transfers between devices, shards(): lax.psum((row_sums[0], row_sums[1], row_sums[2], other_sums[0], other_sum...  103 us
    dot_general x10, matrix products, product(): jnp.einsum(spec_text, left_op, right_op, preferred_element_type=jnp.float32)  43.1 us
    psum x1, blocking collectives, shards(): lax.psum((row_sums[0], row_sums[1], row_sums[2], other_sums[0], other_sum...  41.2 us
    all_to_all x1, waiting for transfers between devices, shards(): lax.all_to_all(tokens, 'cols', split_axis=0, concat_axis=1, tiled=True)  15.2 us
    unnamed x91, local copies, waits for them, and re-layouts  15 us
    dot_general x6, matrix products, over_cells(): lax.dot_general(left_flat, right_flat, (((0,), (0,)), ((), ())), preferre...  13.3 us
    all_to_all x1, blocking collectives, shards(): lax.all_to_all(key_bias, 'cols', split_axis=0, concat_axis=1, tiled=True)  12.1 us
    all_to_all x1, waiting for transfers between devices, shards(): lax.all_to_all(after_rows, 'cols', split_axis=1, concat_axis=0, tiled=True)  10.8 us
  transfers between devices with their start and end apart: 11, of which 7 were waited for; matrix products, arithmetic and copies ran while one was open for 6% of the time, Pallas kernels for 0%

profile of v1, /device:TPU:0, one launch (start us, length us, event | category | flops | bytes accessed | tf_op | source)
XLA Modules:
  0.0 378.1 jit_solution(9285951788832923822)
XLA Ops:
  7.2 12.1 %all_to_all.116 = bf16[8,4,32]{2,1,0:T(4,128)(2,1)S(1)} all-to-all(bf16[8,4,32]{2,1,0:T(4,128)(2,1)} %bitcast.282), channel_id=1, replica_groups=mesh['rows'=4,'cols'=8] {'cols'}, dimensions={0} | all-to-all | bytes 4096 | tf_op jit(solution)/shard_map/all_to_all | solution.py:216
  19.3 3.6 all-to-all-start
  23.0 15.2 %all-to-all-done = bf16[32,32,256]{2,1,0:T(8,128)(2,1)S(1)} async-done(((bf16[32,32,256]{2,1,0:T(8,128)(2,1)}), bf16[32,32,256]{2,1,0:T(8,128)(2,1)S(1)}, u32[]{:S(2)}, u32[]{:S(2)}) %all-to-all-start) | async-done | bytes 524320 | tf_op jit(solution)/shard_map/all_to_all | solution.py:215
  42.5 4.7 %fusion.125 = (f32[4,4,256]{2,1,0:T(4,128)S(1)}, f32[4,4,256,256]{2,3,1,0:T(8,128)}) fusion(f32[4,256]{1,0:T(4,128)S(1)} %reshape.278, bf16[4,256,4,64]{1,3,2,0:T(8,128)(2,1)S(1)} %bitcast.266, bf16[4,256,4,64]{1,3,2,0:T(8,128)(2,1)} %bitcast.264), kind=kOutput, calls=%fused_computation.174 | convolution fusion | flops 138412288 | bytes 5263360 | tf_op jit(solution)/shard_map/while/body/eval_jaxpr/sub | solution.py:95
  47.2 2.7 convolution_convert_fusion.7
  52.3 3.5 all-to-all-start.2
  56.0 1.6 collective-permute-start.1
  60.3 10.8 %all-to-all-done.2 = bf16[4,256,256]{2,0,1:T(4,128)(2,1)S(1)} async-done(((bf16[4,256,256]{2,0,1:T(4,128)(2,1)}), bf16[4,256,256]{2,0,1:T(4,128)(2,1)S(1)}, u32[]{:S(2)}, u32[]{:S(2)}) %all-to-all-start.2) | async-done | bytes 524320 | tf_op jit(solution)/shard_map/all_to_all | solution.py:222
  71.1 3.7 all-to-all-start.4
  76.0 3.4 all-to-all-done.4
  79.4 3.7 all-to-all-start.3
  84.9 4.7 %all-to-all-done.3 = bf16[32,32,256]{2,0,1:T(8,128)(2,1)S(1)} async-done(((bf16[32,32,256]{2,0,1:T(8,128)(2,1)}), bf16[32,32,256]{2,0,1:T(8,128)(2,1)S(1)}, u32[]{:S(2)}, u32[]{:S(2)}) %all-to-all-start.3) | async-done | bytes 524320 | tf_op jit(solution)/shard_map/all_to_all | solution.py:221
  95.8 2.0 copy.399
  100.2 3.7 fusion.126
  103.9 2.0 convolution_convert_fusion.6
  107.7 2.9 multiply_convert_fusion
  110.5 3.2 fusion.10
  116.8 2.0 copy.404
  118.9 3.5 convolution_convert_fusion.5
  122.4 1.8 fusion.127
  124.2 5.2 %fusion.42 = bf16[8,4,64,128]{3,2,1,0:T(8,128)(2,1)} fusion(bf16[128,8,4,64]{0,3,2,1:T(8,128)(2,1)} %bitcast.269, f32[8,4,128,128]{2,3,1,0:T(8,128)} %fusion.127, f32[8,4,128,128]{2,3,1,0:T(8,128)} %get-tuple-element.131, f32[8,4,128]{2,1,0:T(4,128)S(1)} %get-tuple-element.130), kind=kOutput, calls=%fused_computation.50 | convolution fusion | flops 71045248 | bytes 5259264 | tf_op jit(solution)/shard_map/while/body/eval_jaxpr/shqk,kshd->qshd/dot_general | solution.py:33
  129.4 5.2 %fusion.45 = bf16[8,4,64,128]{3,2,1,0:T(8,128)(2,1)} fusion(bf16[128,8,4,64]{0,3,2,1:T(8,128)(2,1)} %bitcast.271, f32[8,4,128,128]{2,3,1,0:T(8,128)} %fusion.127, f32[8,4,128,128]{2,3,1,0:T(8,128)} %get-tuple-element.131, f32[8,4,128]{2,1,0:T(4,128)S(1)} %get-tuple-element.130), kind=kOutput, calls=%fused_computation.51 | convolution fusion | flops 71045248 | bytes 5259264 | tf_op jit(solution)/shard_map/while/body/eval_jaxpr/shqk,qshd->kshd/dot_general | solution.py:33
  134.6 2.0 copy.410
  136.7 2.0 copy.409
  138.7 2.0 copy.408
  140.8 3.2 multiply_reduce_fusion.2
  145.9 4.1 %all-to-all-start.5 = ((bf16[128,8,256]{2,1,0:T(8,128)(2,1)}), bf16[128,8,256]{2,1,0:T(8,128)(2,1)}, u32[]{:S(2)}, u32[]{:S(2)}) async-start(bf16[128,8,256]{2,1,0:T(8,128)(2,1)} %copy.411), calls=%async_computation.5 | async-start | bytes 1048576 | tf_op jit(solution)/shard_map/all_to_all | solution.py:244
  152.4 1.8 copy.428
  156.7 2.0 copy.467
  158.6 3.5 all-to-all-start.6
  162.5 2.3 convolution_multiply_fusion
  164.7 3.0 fusion.56
  167.7 2.0 fusion.38
  169.7 2.4 fusion.39
  172.1 5.3 %all-to-all-done.6 = bf16[32,32,256]{2,1,0:T(8,128)(2,1)S(1)} async-done(((bf16[32,32,256]{2,1,0:T(8,128)(2,1)}), bf16[32,32,256]{2,1,0:T(8,128)(2,1)S(1)}, u32[]{:S(2)}, u32[]{:S(2)}) %all-to-all-start.6) | async-done | bytes 524320 | tf_op jit(solution)/shard_map/all_to_all | solution.py:243
  177.8 3.8 %convolution_convert_fusion.4 = bf16[4,4,64,256]{3,2,1,0:T(8,128)(2,1)} fusion(bf16[4,256,4,64]{1,3,2,0:T(8,128)(2,1)S(1)} %bitcast.249, f32[4,4,256,256]{2,3,1,0:T(8,128)} %get-tuple-element.129, f32[4,4,256]{2,1,0:T(4,128)S(1)} %get-tuple-element.128), kind=kOutput, calls=%fused_computation.56 | convolution fusion | flops 136577024 | bytes 5259264 | tf_op jit(solution)/shard_map/while/body/eval_jaxpr/shqk,sqhd->skhd/dot_general | solution.py:33
  181.6 2.7 fusion.128
  184.4 8.0 %fusion.48 = bf16[4,4,64,256]{3,2,1,0:T(8,128)(2,1)} fusion(bf16[4,256,4,64]{1,3,2,0:T(8,128)(2,1)S(1)} %bitcast.265, f32[4,4,256,256]{2,3,1,0:T(8,128)} %fusion.128, f32[4,4,256,256]{2,3,1,0:T(8,128)} %get-tuple-element.129, f32[4,4,256]{2,1,0:T(4,128)S(1)} %get-tuple-element.128), kind=kOutput, calls=%fused_computation.52 | convolution fusion | flops 141824256 | bytes 9453568 | tf_op jit(solution)/shard_map/while/body/eval_jaxpr/shqk,skhd->sqhd/dot_general | solution.py:33
  192.4 8.0 %fusion.51 = bf16[4,4,64,256]{3,2,1,0:T(8,128)(2,1)} fusion(bf16[4,256,4,64]{1,3,2,0:T(8,128)(2,1)S(1)} %bitcast.267, f32[4,4,256,256]{2,3,1,0:T(8,128)} %fusion.128, f32[4,4,256,256]{2,3,1,0:T(8,128)} %get-tuple-element.129, f32[4,4,256]{2,1,0:T(4,128)S(1)} %get-tuple-element.128), kind=kOutput, calls=%fused_computation.53 | convolution fusion | flops 141824256 | bytes 9453568 | tf_op jit(solution)/shard_map/while/body/eval_jaxpr/shqk,sqhd->skhd/dot_general | solution.py:33
  201.7 2.1 copy.418
  203.9 2.0 copy.417
  206.9 2.7 fusion.57
  214.3 3.5 all-to-all-start.7
  217.9 41.2 %all-reduce = (f32[256]{0:T(256)}, f32[256]{0:T(256)}, f32[256]{0:T(256)}) all-reduce(f32[256]{0:T(256)S(1)} %broadcast_multiply_fusion.11, f32[256]{0:T(256)S(1)} %broadcast_multiply_fusion.10, f32[256]{0:T(256)S(1)} %broadcast_multiply_fusion.9), channel_id=1, replica_groups=mesh['rows'=4,'cols'=8] {'rows','cols'}, use_global_device_ids=true, to_apply=%region_19.20 | all-reduce | flops 768 | bytes 6144 | tf_op jit(solution)/shard_map/psum | solution.py:255
  259.9 102.7 %all-reduce.4.cloned.1.call-done = (f32[256,768]{1,0:T(8,128)}, f32[256,256]{1,0:T(8,128)}, f32[256,768]{1,0:T(8,128)}, f32[256,256]{1,0:T(8,128)}, f32[256,1024]{1,0:T(8,128)}, /*index=5*/f32[1024,256]{1,0:T(8,128)}) async-done(((f32[256,768]{1,0:T(8,128)}, f32[256,256]{1,0:T(8,128)}, f32[256,768]{1,0:T(8,128)}, f32[256,256]{1,0:T(8,128)}, f32[256,1024]{1,0:T(8,128)}, /*index=5*/f32[1024,256]{1,0:T(8,128)}), ...) | async-done | bytes 4194320 | tf_op jit(solution)/shard_map/psum | solution.py:255
  362.6 2.2 copy.474
  364.8 1.7 copy.475
  366.6 2.1 copy.476
  (173 shorter events, 43.8 us)
Async XLA Ops:
  7.2 100.4 %copy-start = (bf16[256,1024]{1,0:T(8,128)(2,1)S(1)}, bf16[256,1024]{1,0:T(8,128)(2,1)}, u32[]{:S(2)}) copy-start(bf16[256,1024]{1,0:T(8,128)(2,1)} %param.22) | copy-start | bytes 1572868
  19.3 19.9 %copy-start.35 = (f32[256]{0:T(256)S(1)}, f32[256]{0:T(256)}, u32[]{:S(2)}) copy-start(f32[256]{0:T(256)} %param.15) | copy-start | bytes 3076
  19.3 18.9 %all-to-all-start = ((bf16[32,32,256]{2,1,0:T(8,128)(2,1)}), bf16[32,32,256]{2,1,0:T(8,128)(2,1)S(1)}, u32[]{:S(2)}, u32[]{:S(2)}) async-start(bf16[32,32,256]{2,1,0:T(8,128)(2,1)} %param.12), calls=%async_computation | async-start | bytes 1048576 | tf_op jit(solution)/shard_map/all_to_all | solution.py:215
  23.0 17.4 %copy-start.29 = (bf16[256,768]{1,0:T(8,128)(2,1)S(1)}, bf16[256,768]{1,0:T(8,128)(2,1)}, u32[]{:S(2)}) copy-start(bf16[256,768]{1,0:T(8,128)(2,1)} %param.16) | copy-start | bytes 1179652
  39.6 0.8 copy-start.9
  42.3 4.9 %copy-start.25 = (bf16[4,256,256]{1,2,0:T(8,128)(2,1)}, bf16[4,256,256]{1,2,0:T(8,128)(2,1)S(1)}, u32[]{:S(2)}) copy-start(bf16[4,256,256]{1,2,0:T(8,128)(2,1)S(1)} %copy.381) | copy-start | bytes 1572868
  42.5 4.7 %copy-start.3 = (bf16[4,256,256]{1,2,0:T(8,128)(2,1)}, bf16[4,256,256]{1,2,0:T(8,128)(2,1)S(1)}, u32[]{:S(2)}) copy-start(bf16[4,256,256]{1,2,0:T(8,128)(2,1)S(1)} %copy.380) | copy-start | bytes 1572868
  47.2 3.5 copy-start.22
  50.0 5.9 %copy-start.23 = (bf16[32,32,256]{2,1,0:T(8,128)(2,1)S(1)}, bf16[32,32,256]{2,1,0:T(8,128)(2,1)}, u32[]{:S(2)}) copy-start(bf16[32,32,256]{2,1,0:T(8,128)(2,1)} %param.14) | copy-start | bytes 1572868
  50.0 9.6 %copy-start.32 = (bf16[32,32]{1,0:T(8,128)(2,1)S(1)}, bf16[32,32]{1,0:T(8,128)(2,1)}, u32[]{:S(2)}) copy-start(bf16[32,32]{1,0:T(8,128)(2,1)} %param.13) | copy-start | bytes 6148
  52.3 18.8 %all-to-all-start.2 = ((bf16[4,256,256]{2,0,1:T(4,128)(2,1)}), bf16[4,256,256]{2,0,1:T(4,128)(2,1)S(1)}, u32[]{:S(2)}, u32[]{:S(2)}) async-start(bf16[4,256,256]{2,0,1:T(4,128)(2,1)} %copy.386), calls=%async_computation.2 | async-start | bytes 1048576 | tf_op jit(solution)/shard_map/all_to_all | solution.py:222
  56.0 27.3 %collective-permute-start.1 = (bf16[32,8,256]{2,1,0:T(8,128)(2,1)S(1)}, bf16[32,8,256]{2,1,0:T(8,128)(2,1)S(1)}, u32[]{:S(2)}, u32[]{:S(2)}) collective-permute-start(bf16[32,8,256]{2,1,0:T(8,128)(2,1)S(1)} %get-tuple-element.125), channel_id=1, source_target_pairs={{0,16},{8,24},{16,0},{24,8},{1,17},{9,25},{17,1},{25,9},{2,18},{10... | collective-permute-start | bytes 393224 | tf_op jit(solution)/shard_map/ppermute | solution.py:27
  57.6 25.7 %collective-permute-start = (bf16[32,8,256]{2,1,0:T(8,128)(2,1)S(1)}, bf16[32,8,256]{2,1,0:T(8,128)(2,1)S(1)}, u32[]{:S(2)}, u32[]{:S(2)}) collective-permute-start(bf16[32,8,256]{2,1,0:T(8,128)(2,1)S(1)} %get-tuple-element.126), channel_id=1, source_target_pairs={{0,8},{8,0},{16,24},{24,16},{1,9},{9,1},{17,25},{25,17},{2,10},{10... | collective-permute-start | bytes 393224 | tf_op jit(solution)/shard_map/ppermute | solution.py:27
  59.0 24.2 %collective-permute-start.2 = (bf16[32,8,256]{2,1,0:T(8,128)(2,1)S(1)}, bf16[32,8,256]{2,1,0:T(8,128)(2,1)S(1)}, u32[]{:S(2)}, u32[]{:S(2)}) collective-permute-start(bf16[32,8,256]{2,1,0:T(8,128)(2,1)S(1)} %get-tuple-element.127), channel_id=1, source_target_pairs={{0,24},{8,16},{16,8},{24,0},{1,25},{9,17},{17,9},{25,1},{2,26},{10... | collective-permute-start | bytes 393224 | tf_op jit(solution)/shard_map/ppermute | solution.py:27
  71.1 8.3 %all-to-all-start.4 = ((bf16[4,2,128]{2,1,0:T(2,128)(2,1)}), bf16[4,2,128]{2,1,0:T(2,128)(2,1)S(1)}, u32[]{:S(2)}, u32[]{:S(2)}) async-start(bf16[4,2,128]{2,1,0:T(2,128)(2,1)} %reshape.302), calls=%async_computation.4 | async-start | bytes 4096 | tf_op jit(solution)/shard_map/all_to_all | solution.py:230
  79.4 10.2 %all-to-all-start.3 = ((bf16[32,32,256]{2,0,1:T(8,128)(2,1)}), bf16[32,32,256]{2,0,1:T(8,128)(2,1)S(1)}, u32[]{:S(2)}, u32[]{:S(2)}) async-start(bf16[32,32,256]{2,0,1:T(8,128)(2,1)} %copy.389), calls=%async_computation.3 | async-start | bytes 1048576 | tf_op jit(solution)/shard_map/all_to_all | solution.py:221
  83.9 7.0 %copy-start.11 = (bf16[4,32,8,256]{3,2,1,0:T(8,128)(2,1)}, bf16[4,32,8,256]{3,2,1,0:T(8,128)(2,1)S(1)}, u32[]{:S(2)}) copy-start(bf16[4,32,8,256]{3,2,1,0:T(8,128)(2,1)S(1)} %gather_fusion) | copy-start | bytes 1572868
  84.0 8.0 %copy-start.34 = (f32[256]{0:T(256)S(1)}, f32[256]{0:T(256)}, u32[]{:S(2)}) copy-start(f32[256]{0:T(256)} %param.18) | copy-start | bytes 3076
  100.2 5.8 %copy-start.16 = (bf16[128,8,256]{0,2,1:T(8,128)(2,1)}, bf16[128,8,256]{0,2,1:T(8,128)(2,1)S(1)}, u32[]{:S(2)}) copy-start(bf16[128,8,256]{0,2,1:T(8,128)(2,1)S(1)} %copy.397) | copy-start | bytes 1572868
  103.9 2.9 copy-start.21
  103.9 3.7 copy-start.33
  107.6 2.9 copy-start.6
  107.7 2.9 copy-start.38
  113.7 2.0 copy-start.7
  118.9 3.5 copy-start.17
  118.9 3.5 copy-start.18
  145.9 10.8 %all-to-all-start.5 = ((bf16[128,8,256]{2,1,0:T(8,128)(2,1)}), bf16[128,8,256]{2,1,0:T(8,128)(2,1)}, u32[]{:S(2)}, u32[]{:S(2)}) async-start(bf16[128,8,256]{2,1,0:T(8,128)(2,1)} %copy.411), calls=%async_computation.5 | async-start | bytes 1048576 | tf_op jit(solution)/shard_map/all_to_all | solution.py:244
  155.7 9.0 %copy-start.14 = (bf16[128,8,256]{2,0,1:T(8,128)(2,1)S(1)}, bf16[128,8,256]{2,0,1:T(8,128)(2,1)}, u32[]{:S(2)}) copy-start(bf16[128,8,256]{2,0,1:T(8,128)(2,1)} %copy-done.13) | copy-start | bytes 1572868
  158.6 18.8 %all-to-all-start.6 = ((bf16[32,32,256]{2,1,0:T(8,128)(2,1)}), bf16[32,32,256]{2,1,0:T(8,128)(2,1)S(1)}, u32[]{:S(2)}, u32[]{:S(2)}) async-start(bf16[32,32,256]{2,1,0:T(8,128)(2,1)} %bitcast.255), calls=%async_computation.6 | async-start | bytes 1048576 | tf_op jit(solution)/shard_map/all_to_all | solution.py:243
  162.1 200.5 %all-reduce.4.cloned.1.call-start = ((), (), s32[]{:S(2)}) async-start(), calls=%async_computation.8 | async-start | bytes 8388608 | tf_op jit(solution)/shard_map/psum | solution.py:255
  164.7 3.0 copy-start.8
  167.7 2.0 copy-start.12
  167.7 2.0 copy-start.39
  177.8 3.8 %copy-start.4 = (bf16[4,256,256]{1,2,0:T(8,128)(2,1)S(1)}, bf16[4,256,256]{1,2,0:T(8,128)(2,1)}, u32[]{:S(2)}) copy-start(bf16[4,256,256]{1,2,0:T(8,128)(2,1)} %copy-done.3) | copy-start | bytes 1572868
  181.6 2.7 copy-start.24
  184.4 8.0 %copy-start.26 = (bf16[4,256,256]{1,2,0:T(8,128)(2,1)S(1)}, bf16[4,256,256]{1,2,0:T(8,128)(2,1)}, u32[]{:S(2)}) copy-start(bf16[4,256,256]{1,2,0:T(8,128)(2,1)} %copy-done.25) | copy-start | bytes 1572868
  200.4 5.5 %copy-start.15 = (bf16[32,8,4,256]{3,1,2,0:T(8,128)(2,1)S(1)}, bf16[32,8,4,256]{3,1,2,0:T(8,128)(2,1)}, u32[]{:S(2)}) copy-start(bf16[32,8,4,256]{3,1,2,0:T(8,128)(2,1)} %copy.450) | copy-start | bytes 1572868
  200.4 6.5 %copy-start.10 = (bf16[4,256,256]{2,1,0:T(8,128)(2,1)S(1)}, bf16[4,256,256]{2,1,0:T(8,128)(2,1)}, u32[]{:S(2)}) copy-start(bf16[4,256,256]{2,1,0:T(8,128)(2,1)} %copy-done.9) | copy-start | bytes 1572868
  209.6 1.0 copy-start.27
  209.6 1.2 copy-start.28
  209.6 1.3 copy-start.30
  212.2 5.6 %copy-start.36 = (f32[256]{0:T(256)S(1)}, f32[256]{0:T(256)}, u32[]{:S(2)}) copy-start(f32[256]{0:T(256)} %get-tuple-element.73) | copy-start | bytes 3076
  212.2 5.6 %copy-start.37 = (f32[256]{0:T(256)S(1)}, f32[256]{0:T(256)}, u32[]{:S(2)}) copy-start(f32[256]{0:T(256)} %get-tuple-element.84) | copy-start | bytes 3076
  214.3 44.7 %all-to-all-start.7 = ((bf16[4,256,256]{2,0,1:T(4,128)(2,1)}), bf16[4,256,256]{2,0,1:T(4,128)(2,1)S(1)}, u32[]{:S(2)}, u32[]{:S(2)}) async-start(bf16[4,256,256]{2,0,1:T(4,128)(2,1)} %copy.421), calls=%async_computation.7 | async-start | bytes 1048576 | tf_op jit(solution)/shard_map/all_to_all | solution.py:253
  362.6 6.0 %copy-start.31 = (f32[256,256]{1,0:T(8,128)S(1)}, f32[256,256]{1,0:T(8,128)}, u32[]{:S(2)}) copy-start(f32[256,256]{1,0:T(8,128)} %get-tuple-element.147) | copy-start | bytes 786436
  362.6 6.7 %copy-start.20 = (f32[256,1024]{1,0:T(8,128)S(1)}, f32[256,1024]{1,0:T(8,128)}, u32[]{:S(2)}) copy-start(f32[256,1024]{1,0:T(8,128)} %get-tuple-element.149) | copy-start | bytes 3145732
  362.6 7.7 %copy-start.19 = (f32[1024,256]{1,0:T(8,128)S(1)}, f32[1024,256]{1,0:T(8,128)}, u32[]{:S(2)}) copy-start(f32[1024,256]{1,0:T(8,128)} %get-tuple-element.150) | copy-start | bytes 3145732
  364.8 6.4 %copy-start.1 = (bf16[256,1024]{1,0:T(8,128)(2,1)S(1)}, bf16[256,1024]{1,0:T(8,128)(2,1)}, u32[]{:S(2)}) copy-start(bf16[256,1024]{1,0:T(8,128)(2,1)} %param.22) | copy-start | bytes 1572868
  (3 other events, 2.4 us)
Sparse Core Ops, SparseCore 0:
  209.8 152.8 all-reduce.3
